TPU v7x, 256 devices: a whole 4x4x8 slice. The times are simulated.
256 devices in a mesh: dp: 8 (over x, z_hi), tensor: 8 (over y, core), expert: 4 (over z_lo).
Axes of the slice: x: 4, y: 4, z: 8 (z_hi: 2, z_lo: 4; z = z_hi * 4 + z_lo), core: 2. Of those that a mesh axis runs over, the one named last changes fastest.
Arguments:
- moe_input: bfloat16 [8192, 2048], P(('dp', 'tensor'), 'expert'), may hold values from -6 to 6
- grad_output: bfloat16 [8192, 2048], P(('dp', 'tensor'), 'expert'), may hold values from -6 to 6
- routes: int32 [8192, 8], P(('dp', 'tensor')), may hold values from 0 to 127, all different within a row; in each aligned block of 128 rows (0 to 127, 128 to 255, ...) at most 12 rows name the same one
- route_weight: float32 [8192, 8], P(('dp', 'tensor')), may hold values from 0.05 to 0.35
- capacity: int32 [128], replicated, may hold values from 6 to 12, as said below
- w_gate: bfloat16 [256, 384, 2048], P(('dp', 'tensor', 'expert')), may hold values from -0.125 to 0.125
- w_up: bfloat16 [256, 384, 2048], P(('dp', 'tensor', 'expert')), may hold values from -0.125 to 0.125
- w_down: bfloat16 [256, 384, 2048], P(('dp', 'tensor', 'expert')), may hold values from -0.21875 to 0.21875
Outputs:
- moe_output: bfloat16 [8192, 2048], P(('dp', 'tensor'), 'expert')
- grad_input: bfloat16 [8192, 2048], P(('dp', 'tensor'), 'expert')
- grad_gate: bfloat16 [256, 384, 2048], P(('dp', 'tensor', 'expert'))
- grad_up: bfloat16 [256, 384, 2048], P(('dp', 'tensor', 'expert'))
- grad_down: bfloat16 [256, 384, 2048], P(('dp', 'tensor', 'expert'))
Inputs may be any that keep to these rules, and one draw needn't show every extreme that they name: `routes`: each row names 8 different experts; within each aligned block of 128 rows (the rows of one device) no expert is named more than 12 times. Some expert has a capacity of exactly 12.
All inputs are finite; a program needn't handle non-finite values.
Results may differ from a plain program's by a relative error of at most 0.0071.
Values may be sent and summed in bfloat16 or wider, within the bound.
A program may use at most 128 MiB of HBM per device.

v0:
```python
import jax
import jax.numpy as jnp
from jax import lax
from jax.sharding import PartitionSpec as P


def swapped(x, axis, apart):
    return lax.ppermute(x, axis, [(i, i ^ 1 << apart) for i in range(lax.axis_size(axis))])


def expert_work(slot_rows, slot_cots, gate_w, up_w, down_w):
    gate_pre = jnp.einsum("smd,hd->smh", slot_rows, gate_w, preferred_element_type=jnp.float32)
    up_pre = jnp.einsum("smd,hd->smh", slot_rows, up_w, preferred_element_type=jnp.float32)
    sigmoid_gate = jax.nn.sigmoid(gate_pre)
    gate_act = gate_pre * sigmoid_gate
    hidden = (gate_act * up_pre).astype(jnp.bfloat16)
    out_part = jnp.einsum("smh,hd->smd", hidden, down_w, preferred_element_type=jnp.float32).astype(
        jnp.bfloat16
    )
    hidden_cot = jnp.einsum("smd,hd->smh", slot_cots, down_w, preferred_element_type=jnp.float32)
    gate_cot = (
        hidden_cot * up_pre * sigmoid_gate * (1.0 + gate_pre * (1.0 - sigmoid_gate))
    ).astype(jnp.bfloat16)
    up_cot = (hidden_cot * gate_act).astype(jnp.bfloat16)
    in_sum = jnp.einsum("smh,hd->smd", gate_cot, gate_w, preferred_element_type=jnp.float32)
    in_sum = in_sum + jnp.einsum("smh,hd->smd", up_cot, up_w, preferred_element_type=jnp.float32)
    in_part = in_sum.astype(jnp.bfloat16)
    grad_gate = jnp.einsum(
        "smh,smd->hd", gate_cot, slot_rows, preferred_element_type=jnp.float32
    ).astype(jnp.bfloat16)
    grad_up = jnp.einsum(
        "smh,smd->hd", up_cot, slot_rows, preferred_element_type=jnp.float32
    ).astype(jnp.bfloat16)
    grad_down = jnp.einsum(
        "smh,smd->hd", hidden, slot_cots, preferred_element_type=jnp.float32
    ).astype(jnp.bfloat16)
    return (out_part, in_part, grad_gate[None], grad_up[None], grad_down[None])


def fill_slots(inputs, cots, owners, weights):
    filled = owners >= 0
    source = jnp.maximum(owners, 0)
    slot_rows = jnp.where(filled[..., None], inputs[source], jnp.zeros((), inputs.dtype))
    slot_cots = jnp.where(
        filled[..., None], weights[..., None] * cots[source].astype(jnp.float32), 0.0
    )
    return (slot_rows, slot_cots.astype(jnp.bfloat16))


def shards(moe_input, grad_output, routes, route_weight, capacity, w_gate, w_up, w_down):
    groups = lax.axis_size(("dp", "tensor"))
    position = lax.axis_index("expert")
    parity = position // 2
    half_index = position % 2
    tok_rows = routes.shape[0]
    topk = routes.shape[1]
    experts = capacity.shape[0]
    slot_depth = 12 * tok_rows // experts
    slot_count = experts * slot_depth
    pair_count = tok_rows * topk
    col_quarter = moe_input.shape[1]
    full_width = col_quarter * lax.axis_size("expert")
    half_width = full_width // 2
    flat_routes = routes.reshape(pair_count)
    onehot = (flat_routes[:, None] == jnp.arange(experts, dtype=jnp.int32)[None, :]).astype(
        jnp.int32
    )
    before = jnp.cumsum(onehot, axis=0) - onehot
    pair_rank = jnp.sum(onehot * before, axis=1)
    pair_limit = jnp.sum(onehot * capacity[None, :], axis=1)
    pair_kept = pair_rank < pair_limit
    pair_place = jnp.where(pair_kept, flat_routes * slot_depth + pair_rank, slot_count)
    pair_token = jnp.arange(pair_count, dtype=jnp.int32) // topk
    flat_weight = route_weight.reshape(pair_count)
    slot_owner = jnp.full((slot_count,), -1, jnp.int32).at[pair_place].set(pair_token, mode="drop")
    slot_weight = jnp.zeros((slot_count,), jnp.float32).at[pair_place].set(flat_weight, mode="drop")
    whole_input, whole_cot = (
        lax.all_gather(moe_input, "expert", axis=1, tiled=True),
        lax.all_gather(grad_output, "expert", axis=1, tiled=True),
    )
    owners = lax.dynamic_index_in_dim(
        slot_owner.reshape(groups, 2, slot_depth), parity, 1, keepdims=False
    )
    weights = lax.dynamic_index_in_dim(
        slot_weight.reshape(groups, 2, slot_depth), parity, 1, keepdims=False
    )
    send_rows, send_cots = fill_slots(whole_input, whole_cot, owners, weights)
    got_rows, got_cots = (
        lax.all_to_all(send_rows, ("dp", "tensor"), split_axis=0, concat_axis=0, tiled=True),
        lax.all_to_all(send_cots, ("dp", "tensor"), split_axis=0, concat_axis=0, tiled=True),
    )
    out_part, in_part, grad_gate, grad_up, grad_down = expert_work(
        got_rows, got_cots, w_gate[0], w_up[0], w_down[0]
    )
    out_split = out_part.reshape(groups, slot_depth, 2, half_width)
    in_split = in_part.reshape(groups, slot_depth, 2, half_width)
    mine_out = lax.dynamic_index_in_dim(out_split, half_index, 2, keepdims=False)
    mine_in = lax.dynamic_index_in_dim(in_split, half_index, 2, keepdims=False)
    other_out = lax.dynamic_index_in_dim(out_split, 1 - half_index, 2, keepdims=False)
    other_in = lax.dynamic_index_in_dim(in_split, 1 - half_index, 2, keepdims=False)
    peer_out, peer_in = swapped((other_out, other_in), "expert", 0)
    expert_out = (mine_out.astype(jnp.float32) + peer_out.astype(jnp.float32)).astype(jnp.bfloat16)
    input_slot = (mine_in.astype(jnp.float32) + peer_in.astype(jnp.float32)).astype(jnp.bfloat16)
    back_out, back_in = (
        lax.all_to_all(expert_out, ("dp", "tensor"), split_axis=0, concat_axis=0, tiled=True),
        lax.all_to_all(input_slot, ("dp", "tensor"), split_axis=0, concat_axis=0, tiled=True),
    )
    flat_out = back_out.reshape(groups * slot_depth, half_width)
    flat_in = back_in.reshape(groups * slot_depth, half_width)
    matched = pair_kept & (flat_routes % 2 == parity)
    back_place = jnp.where(matched, flat_routes // 2 * slot_depth + pair_rank, 0)
    pair_scale = jnp.where(matched, flat_weight, 0.0)
    pair_mask = jnp.where(matched, 1.0, 0.0)
    partial_out = jnp.sum(
        (flat_out[back_place].astype(jnp.float32) * pair_scale[:, None]).reshape(
            tok_rows, topk, half_width
        ),
        axis=1,
    )
    partial_in = jnp.sum(
        (flat_in[back_place].astype(jnp.float32) * pair_mask[:, None]).reshape(
            tok_rows, topk, half_width
        ),
        axis=1,
    )
    which_half = (jnp.arange(2, dtype=jnp.int32) == half_index)[None, :, None]
    placed_out = jnp.where(which_half, partial_out[:, None, :], 0.0).reshape(tok_rows, full_width)
    placed_in = jnp.where(which_half, partial_in[:, None, :], 0.0).reshape(tok_rows, full_width)
    moe_output, grad_input = (
        lax.psum_scatter(placed_out, "expert", scatter_dimension=1, tiled=True),
        lax.psum_scatter(placed_in, "expert", scatter_dimension=1, tiled=True),
    )
    return (
        moe_output.astype(jnp.bfloat16),
        grad_input.astype(jnp.bfloat16),
        grad_gate,
        grad_up,
        grad_down,
    )


def solution(mesh):
    in_specs = (
        P(("dp", "tensor"), "expert"),
        P(("dp", "tensor"), "expert"),
        P(("dp", "tensor"), None),
        P(("dp", "tensor"), None),
        P(),
        P(("dp", "tensor", "expert"), None, None),
        P(("dp", "tensor", "expert"), None, None),
        P(("dp", "tensor", "expert"), None, None),
    )
    out_specs = (
        P(("dp", "tensor"), "expert"),
        P(("dp", "tensor"), "expert"),
        P(("dp", "tensor", "expert"), None, None),
        P(("dp", "tensor", "expert"), None, None),
        P(("dp", "tensor", "expert"), None, None),
    )
    return jax.shard_map(shards, mesh=mesh, in_specs=in_specs, out_specs=out_specs, check_vma=False)
```

profile of v0, /device:TPU:1, one launch (start us, length us, event | category | flops | bytes accessed | tf_op | source)
XLA Modules:
  0.0 627.3 jit_solution(496338516431408893)
XLA Ops:
  7.2 0.9 copy.60
  9.0 1.2 select_reduce_fusion
  10.2 4.3 scatter_custom_fusion
  15.0 16.3 %all_gather.6 = bf16[128,2048]{1,0:T(8,128)(2,1)S(1)} all-gather(bf16[128,512]{1,0:T(8,128)(2,1)S(1)} %copy-done.8), channel_id=1, replica_groups=mesh['dp'=8,'tensor'=8,'expert'=4] {'expert'}, dimensions={1}, use_global_device_ids=true | all-gather | bytes 655360 | tf_op jit(solution)/shard_map/all_gather | solution.py:78
  31.3 4.2 gather_fusion
  35.6 6.1 reshape.310
  41.7 4.5 broadcast_select_fusion
  46.2 15.3 %all-to-all-start = ((bf16[64,12,2048]{2,1,0:T(8,128)(2,1)}), bf16[64,12,2048]{2,1,0:T(8,128)(2,1)}, u32[]{:S(2)}, u32[]{:S(2)}) async-start(bf16[64,12,2048]{2,1,0:T(8,128)(2,1)} %broadcast_select_fusion), calls=%async_computation | async-start | bytes 8388608 | tf_op jit(solution)/shard_map/all_to_all | solution.py:89
  61.7 4.3 scatter_custom_fusion.1
  66.2 97.9 %all_gather.7 = bf16[128,2048]{1,0:T(8,128)(2,1)S(1)} all-gather(bf16[128,512]{1,0:T(8,128)(2,1)S(1)} %copy-done.9), channel_id=1, replica_groups=mesh['dp'=8,'tensor'=8,'expert'=4] {'expert'}, dimensions={1}, use_global_device_ids=true | all-gather | bytes 655360 | tf_op jit(solution)/shard_map/all_gather | solution.py:79
  164.1 4.3 gather_fusion.2
  168.4 6.4 %reshape.361 = f32[64,12,2048]{2,1,0:T(8,128)} reshape(bf16[768,2048]{1,0:T(8,128)(2,1)} %gather_fusion.2) | data formatting | bytes 9437184 | tf_op jit(solution)/shard_map/convert_element_type | solution.py:45
  174.8 5.2 select_convert_fusion
  180.1 13.6 %all-to-all-start.2 = ((bf16[64,12,2048]{2,1,0:T(8,128)(2,1)}), bf16[64,12,2048]{2,1,0:T(8,128)(2,1)}, u32[]{:S(2)}, u32[]{:S(2)}) async-start(bf16[64,12,2048]{2,1,0:T(8,128)(2,1)} %select_convert_fusion), calls=%async_computation.3 | async-start | bytes 8388608 | tf_op jit(solution)/shard_map/all_to_all | solution.py:90
  193.7 5.8 fusion.13
  199.6 5.2 fusion.17
  204.8 87.0 %all-to-all-done.2 = bf16[64,12,2048]{2,1,0:T(8,128)(2,1)} async-done(((bf16[64,12,2048]{2,1,0:T(8,128)(2,1)}), bf16[64,12,2048]{2,1,0:T(8,128)(2,1)}, u32[]{:S(2)}, u32[]{:S(2)}) %all-to-all-start.2) | async-done | bytes 3145760 | tf_op jit(solution)/shard_map/all_to_all | solution.py:90
  291.8 6.2 multiply_convert_fusion
  298.8 3.5 convolution_convert_fusion
  302.4 6.3 %reshape.299 = bf16[64,12,2,1024]{3,2,0,1:T(2,128)(2,1)} reshape(bf16[64,12,2048]{2,0,1:T(8,128)(2,1)} %convolution_convert_fusion) | data formatting | bytes 6291456 | tf_op jit(solution)/shard_map/reshape | solution.py:95
  308.7 1.8 fusion.15
  310.5 3.5 add_convert_fusion
  314.0 6.1 reshape.303
  320.2 27.6 %constant_dynamic-slice_fusion.1 = (bf16[64,12,1,1024]{3,2,0,1:T(2,128)(2,1)}, bf16[64,12,1,1024]{3,2,0,1:T(2,128)(2,1)}, bf16[64,12,1,1024]{3,2,0,1:T(2,128)(2,1)S(1)}, bf16[64,12,1,1024]{3,2,0,1:T(2,128)(2,1)S(1)}) fusion(bf16[64,12,2,1024]{3,2,0,1:T(2,128)(2,1)} %reshape.303, s32[]{:T(128)S(6)} %select_n.147, s32[]{:T(128)S(6)} %select_n.148, ...), kind=kLoop, calls=%fused_computation.96 | loop fusion | bytes 12582920 | tf_op jit(solution)/shard_map/jit(dynamic_index_in_dim)/dynamic_slice | solution.py:98
  348.4 33.5 %collective-permute-done = bf16[64,12,1024]{2,0,1:T(8,128)(2,1)S(1)} collective-permute-done((bf16[64,12,1024]{2,0,1:T(8,128)(2,1)S(1)}, bf16[64,12,1024]{2,0,1:T(8,128)(2,1)S(1)}, u32[]{:S(2)}, u32[]{:S(2)}) %collective-permute-start) | collective-permute-done | bytes 1572896 | tf_op jit(solution)/shard_map/ppermute | solution.py:8
  382.0 1.1 fusion.3
  383.1 2.2 copy.71
  385.3 8.7 %all-to-all-start.1 = ((bf16[64,12,1024]{2,1,0:T(8,128)(2,1)}), bf16[64,12,1024]{2,1,0:T(8,128)(2,1)}, u32[]{:S(2)}, u32[]{:S(2)}) async-start(bf16[64,12,1024]{2,1,0:T(8,128)(2,1)} %copy.71), calls=%async_computation.1 | async-start | bytes 4194304 | tf_op jit(solution)/shard_map/all_to_all | solution.py:105
  394.0 2.6 copy.135
  396.8 76.5 %collective-permute-done.1 = bf16[64,12,1024]{2,0,1:T(8,128)(2,1)S(1)} collective-permute-done((bf16[64,12,1024]{2,0,1:T(8,128)(2,1)S(1)}, bf16[64,12,1024]{2,0,1:T(8,128)(2,1)S(1)}, u32[]{:S(2)}, u32[]{:S(2)}) %collective-permute-start.1) | collective-permute-done | bytes 1572896 | tf_op jit(solution)/shard_map/ppermute | solution.py:8
  473.3 1.1 fusion.2
  474.4 2.2 copy.84
  476.6 13.5 %all-to-all-start.3 = ((bf16[64,12,1024]{2,1,0:T(8,128)(2,1)}), bf16[64,12,1024]{2,1,0:T(8,128)(2,1)}, u32[]{:S(2)}, u32[]{:S(2)}) async-start(bf16[64,12,1024]{2,1,0:T(8,128)(2,1)} %copy.84), calls=%async_computation.4 | async-start | bytes 4194304 | tf_op jit(solution)/shard_map/all_to_all | solution.py:106
  490.7 2.5 reshape.300
  493.2 5.4 gather_fusion.1
  498.5 2.9 fusion.1
  502.2 32.8 %all-to-all-done.3 = bf16[64,12,1024]{2,1,0:T(8,128)(2,1)} async-done(((bf16[64,12,1024]{2,1,0:T(8,128)(2,1)}), bf16[64,12,1024]{2,1,0:T(8,128)(2,1)}, u32[]{:S(2)}, u32[]{:S(2)}) %all-to-all-start.3) | async-done | bytes 1572896 | tf_op jit(solution)/shard_map/all_to_all | solution.py:106
  535.0 2.5 reshape.304
  537.5 5.4 gather_fusion.3
  542.9 2.9 fusion
  546.5 1.5 broadcast_select_fusion.1
  548.9 7.4 %fusion.6 = bf16[1,384,2048]{2,1,0:T(8,128)(2,1)} fusion(bf16[64,12,384]{2,0,1:T(8,128)(2,1)S(1)} %copy-done.13, bf16[64,12,2048]{2,1,0:T(8,128)(2,1)} %all-to-all-done.2), kind=kOutput, calls=%fused_computation.23 | convolution fusion | flops 1208745984 | bytes 5308416 | tf_op jit(solution)/shard_map/smh,smd->hd/dot_general | solution.py:34
  556.3 7.4 %fusion.5 = bf16[1,384,2048]{2,1,0:T(8,128)(2,1)} fusion(bf16[64,12,384]{2,0,1:T(8,128)(2,1)S(1)} %copy-done.7, bf16[64,12,2048]{2,1,0:T(8,128)(2,1)} %all-to-all-done), kind=kOutput, calls=%fused_computation.22 | convolution fusion | flops 1208745984 | bytes 5308416 | tf_op jit(solution)/shard_map/smh,smd->hd/dot_general | solution.py:31
  563.7 7.5 %fusion.4 = bf16[1,384,2048]{2,1,0:T(8,128)(2,1)} fusion(bf16[64,12,384]{2,0,1:T(8,128)(2,1)S(1)} %get-tuple-element.14, bf16[64,12,2048]{2,1,0:T(8,128)(2,1)} %all-to-all-done), kind=kOutput, calls=%fused_computation.21 | convolution fusion | flops 1208745984 | bytes 5308416 | tf_op jit(solution)/shard_map/smh,smd->hd/dot_general | solution.py:28
  571.2 13.1 %reduce-scatter.5.cloned.1.call-done = f32[128,512]{1,0:T(8,128)} async-done(((f32[128,2048]{1,0:T(8,128)}), f32[128,512]{1,0:T(8,128)}) %reduce-scatter.5.cloned.1.call-update) | async-done | bytes 262160 | tf_op jit(solution)/shard_map/reduce_scatter | solution.py:131
  584.4 1.6 convert_element_type.103
  586.0 32.5 %reduce-scatter.3.cloned.1.call-done = f32[128,512]{1,0:T(8,128)} async-done(((f32[128,2048]{1,0:T(8,128)}), f32[128,512]{1,0:T(8,128)}) %reduce-scatter.3.cloned.1.call-update) | async-done | bytes 262160 | tf_op jit(solution)/shard_map/reduce_scatter | solution.py:130
  618.5 1.6 convert_element_type.91
  (73 shorter events, 5.9 us)
Async XLA Ops:
  7.2 284.6 %copy-start = (bf16[1,384,2048]{2,1,0:T(8,128)(2,1)S(1)}, bf16[1,384,2048]{2,1,0:T(8,128)(2,1)}, u32[]{:S(2)}) copy-start(bf16[1,384,2048]{2,1,0:T(8,128)(2,1)} %param.15) | copy-start | bytes 4718596
  7.2 7.8 %copy-start.8 = (bf16[128,512]{1,0:T(8,128)(2,1)S(1)}, bf16[128,512]{1,0:T(8,128)(2,1)}, u32[]{:S(2)}) copy-start(bf16[128,512]{1,0:T(8,128)(2,1)} %param.8) | copy-start | bytes 393220
  46.2 15.3 %copy-start.11 = (f32[128,8]{0,1:T(8,128)S(1)}, f32[128,8]{0,1:T(8,128)}, u32[]{:S(2)}) copy-start(f32[128,8]{0,1:T(8,128)} %param.11) | copy-start | bytes 12292
  46.2 20.0 %copy-start.9 = (bf16[128,512]{1,0:T(8,128)(2,1)S(1)}, bf16[128,512]{1,0:T(8,128)(2,1)}, u32[]{:S(2)}) copy-start(bf16[128,512]{1,0:T(8,128)(2,1)} %param.9) | copy-start | bytes 393220
  46.2 133.9 %all-to-all-start = ((bf16[64,12,2048]{2,1,0:T(8,128)(2,1)}), bf16[64,12,2048]{2,1,0:T(8,128)(2,1)}, u32[]{:S(2)}, u32[]{:S(2)}) async-start(bf16[64,12,2048]{2,1,0:T(8,128)(2,1)} %broadcast_select_fusion), calls=%async_computation | async-start | bytes 8388608 | tf_op jit(solution)/shard_map/all_to_all | solution.py:89
  180.1 111.7 %all-to-all-start.2 = ((bf16[64,12,2048]{2,1,0:T(8,128)(2,1)}), bf16[64,12,2048]{2,1,0:T(8,128)(2,1)}, u32[]{:S(2)}, u32[]{:S(2)}) async-start(bf16[64,12,2048]{2,1,0:T(8,128)(2,1)} %select_convert_fusion), calls=%async_computation.3 | async-start | bytes 8388608 | tf_op jit(solution)/shard_map/all_to_all | solution.py:90
  193.7 5.9 copy-start.3
  298.0 0.8 copy-start.12
  302.4 6.3 %copy-start.4 = (bf16[1,384,2048]{2,1,0:T(8,128)(2,1)S(1)}, bf16[1,384,2048]{2,1,0:T(8,128)(2,1)}, u32[]{:S(2)}) copy-start(bf16[1,384,2048]{2,1,0:T(8,128)(2,1)} %param.13) | copy-start | bytes 4718596
  308.7 1.8 copy-start.5
  308.7 1.8 copy-start.6
  348.3 33.6 %collective-permute-start = (bf16[64,12,1024]{2,0,1:T(8,128)(2,1)S(1)}, bf16[64,12,1024]{2,0,1:T(8,128)(2,1)S(1)}, u32[]{:S(2)}, u32[]{:S(2)}) collective-permute-start(bf16[64,12,1024]{2,0,1:T(8,128)(2,1)S(1)} %bitcast.99), channel_id=1, source_target_pairs={{0,1},{1,0},{2,3},{3,2},{4,5},{5,4},{6,7},{7,6},{8,9},{9,8},{10,11... | collective-permute-start | bytes 4718600 | tf_op jit(solution)/shard_map/ppermute | solution.py:8
  385.3 91.3 %all-to-all-start.1 = ((bf16[64,12,1024]{2,1,0:T(8,128)(2,1)}), bf16[64,12,1024]{2,1,0:T(8,128)(2,1)}, u32[]{:S(2)}, u32[]{:S(2)}) async-start(bf16[64,12,1024]{2,1,0:T(8,128)(2,1)} %copy.71), calls=%async_computation.1 | async-start | bytes 4194304 | tf_op jit(solution)/shard_map/all_to_all | solution.py:105
  394.0 79.3 %copy-start.2 = (bf16[64,12,1,1024]{3,2,0,1:T(2,128)(2,1)S(1)}, bf16[64,12,1,1024]{3,2,0,1:T(2,128)(2,1)}, u32[]{:S(2)}) copy-start(bf16[64,12,1,1024]{3,2,0,1:T(2,128)(2,1)} %get-tuple-element.9) | copy-start | bytes 4718596
  396.7 76.6 %collective-permute-start.1 = (bf16[64,12,1024]{2,0,1:T(8,128)(2,1)S(1)}, bf16[64,12,1024]{2,0,1:T(8,128)(2,1)S(1)}, u32[]{:S(2)}, u32[]{:S(2)}) collective-permute-start(bf16[64,12,1024]{2,0,1:T(8,128)(2,1)S(1)} %bitcast.100), channel_id=1, source_target_pairs={{0,1},{1,0},{2,3},{3,2},{4,5},{5,4},{6,7},{7,6},{8,9},{9,8},{10,11... | collective-permute-start | bytes 4718600 | tf_op jit(solution)/shard_map/ppermute | solution.py:8
  474.4 16.0 %copy-start.10 = (s32[128,8]{0,1:T(8,128)S(1)}, s32[128,8]{0,1:T(8,128)}, u32[]{:S(2)}) copy-start(s32[128,8]{0,1:T(8,128)} %param.10) | copy-start | bytes 12292
  476.6 58.4 %all-to-all-start.3 = ((bf16[64,12,1024]{2,1,0:T(8,128)(2,1)}), bf16[64,12,1024]{2,1,0:T(8,128)(2,1)}, u32[]{:S(2)}, u32[]{:S(2)}) async-start(bf16[64,12,1024]{2,1,0:T(8,128)(2,1)} %copy.84), calls=%async_computation.4 | async-start | bytes 4194304 | tf_op jit(solution)/shard_map/all_to_all | solution.py:106
  490.2 94.2 %reduce-scatter.5.cloned.1.call-start = ((), (), s32[]{:S(2)}) async-start(), calls=%async_computation.7 | async-start | bytes 1310720 | tf_op jit(solution)/shard_map/reduce_scatter | solution.py:131
  546.5 2.3 copy-start.13
  548.1 70.4 %reduce-scatter.3.cloned.1.call-start = ((), (), s32[]{:S(2)}) async-start(), calls=%async_computation.6 | async-start | bytes 1310720 | tf_op jit(solution)/shard_map/reduce_scatter | solution.py:130
  548.9 7.5 %copy-start.7 = (bf16[64,12,384]{2,0,1:T(8,128)(2,1)S(1)}, bf16[64,12,384]{2,0,1:T(8,128)(2,1)}, u32[]{:S(2)}) copy-start(bf16[64,12,384]{2,0,1:T(8,128)(2,1)} %get-tuple-element.13) | copy-start | bytes 1769476
  563.7 56.4 %copy-start.1 = (bf16[1,384,2048]{2,1,0:T(8,128)(2,1)S(1)}, bf16[1,384,2048]{2,1,0:T(8,128)(2,1)}, u32[]{:S(2)}) copy-start(bf16[1,384,2048]{2,1,0:T(8,128)(2,1)} %param.15) | copy-start | bytes 4718596
Sparse Core Ops, SparseCore 0:
  548.2 36.1 reduce-scatter.4
  587.1 31.3 reduce-scatter.2
where the time goes:
time: 635 us; the launch traced here: 627 us
  waiting for transfers between devices  276 us (43%)
  blocking collectives  114 us (18%)
  local copies, waits for them, and re-layouts  97.8 us (15%)
  starting transfers between devices  51.7 us (8%)
  matrix products  48.5 us (8%)
  other arithmetic  24.3 us (4%)
  between operations  14.9 us (2%)
    ppermute x2, waiting for transfers between devices, swapped(): lax.ppermute(x, axis, [(i, i ^ 1 << apart) for i in range(lax.axis_size(a...  110 us
    all_gather x1, blocking collectives, shards(): lax.all_gather(grad_output, 'expert', axis=1, tiled=True)  97.9 us
    all_to_all x1, waiting for transfers between devices, shards(): lax.all_to_all(send_cots, ('dp', 'tensor'), split_axis=0, concat_axis=0,...  87 us
    all_to_all x1, waiting for transfers between devices, shards(): lax.all_to_all(input_slot, ('dp', 'tensor'), split_axis=0, concat_axis=0,...  32.8 us
    reduce_scatter x1, waiting for transfers between devices, shards(): lax.psum_scatter(placed_out, 'expert', scatter_dimension=1, tiled=True)  32.5 us
    dynamic_slice x1, local copies, waits for them, and re-layouts, shards(): mine_in = lax.dynamic_index_in_dim(in_split, half_index, 2, keepdims=False)  27.6 us
    all_gather x1, blocking collectives, shards(): lax.all_gather(moe_input, 'expert', axis=1, tiled=True)  16.3 us
    all_to_all x1, starting transfers between devices, shards(): lax.all_to_all(send_rows, ('dp', 'tensor'), split_axis=0, concat_axis=0,...  15.3 us
  transfers between devices with their start and end apart: 8, of which 6 were waited for; matrix products, arithmetic and copies ran while one was open for 12% of the time, Pallas kernels for 0%

commit v1 on v0

--- a/solution.py
+++ b/solution.py
@@ -76,7 +76,10 @@
     slot_weight = jnp.zeros((slot_count,), jnp.float32).at[pair_place].set(flat_weight, mode="drop")
     whole_input, whole_cot = (
         lax.all_gather(moe_input, "expert", axis=1, tiled=True),
-        lax.all_gather(grad_output, "expert", axis=1, tiled=True),
+        jnp.concatenate(
+            lax.all_to_all(jnp.stack([grad_output] * lax.axis_size("expert")), "expert", 0, 0),
+            axis=1,
+        ),
     )
     owners = lax.dynamic_index_in_dim(
         slot_owner.reshape(groups, 2, slot_depth), parity, 1, keepdims=False

time: 635 us -> 610 us (0.961)
  blocking collectives: 114 us -> 15.3 us
  starting transfers between devices: 51.7 us -> 95.8 us
  waiting for transfers between devices: 276 us -> 305 us
    all_gather x1 -> x0, blocking collectives: 97.9 us -> none  [shards(): lax.all_gather(grad_output, 'expert', axis=1, tiled=True)]
    all_to_all x1, waiting for transfers between devices: 0.01 us -> 74.5 us  [shards(): lax.all_to_all(send_rows, ('dp', 'tensor'), split_axis=0, concat_axis=0,...]
    all_to_all x1, waiting for transfers between devices: 87 us -> 43.9 us  [shards(): lax.all_to_all(send_cots, ('dp', 'tensor'), split_axis=0, concat_axis=0,...]
    ppermute x2, starting transfers between devices: 0.19 us -> 38.6 us  [swapped(): lax.ppermute(x, axis, [(i, i ^ 1 << apart) for i in range(lax.axis_size(a...]
    all_to_all x0 -> x1, starting transfers between devices: none -> 6.44 us  [shards(): lax.all_to_all(jnp.stack([grad_output] * lax.axis_size('expert')), 'exper...]
  transfers between devices with their start and end apart: 8 -> 9, of which waited for: 6 -> 7; matrix products, arithmetic and copies ran while one was open for 12% -> 16% of each run, Pallas kernels for 0% -> 0%
where the time goes in v1:
time: 610 us; the launch traced here: 602 us
  waiting for transfers between devices  305 us (50%)
  local copies, waits for them, and re-layouts  99.5 us (16%)
  starting transfers between devices  95.8 us (16%)
  matrix products  47.7 us (8%)
  other arithmetic  23.6 us (4%)
  blocking collectives  15.3 us (3%)
  between operations  14.9 us (2%)
    ppermute x2, waiting for transfers between devices, swapped(): lax.ppermute(x, axis, [(i, i ^ 1 << apart) for i in range(lax.axis_size(a...  108 us
    all_to_all x1, waiting for transfers between devices, shards(): lax.all_to_all(send_rows, ('dp', 'tensor'), split_axis=0, concat_axis=0,...  74.5 us
    all_to_all x1, waiting for transfers between devices, shards(): lax.all_to_all(send_cots, ('dp', 'tensor'), split_axis=0, concat_axis=0,...  43.9 us
    ppermute x2, starting transfers between devices, swapped(): lax.ppermute(x, axis, [(i, i ^ 1 << apart) for i in range(lax.axis_size(a...  38.6 us
    all_to_all x1, waiting for transfers between devices, shards(): lax.all_to_all(input_slot, ('dp', 'tensor'), split_axis=0, concat_axis=0,...  37.6 us
    reduce_scatter x1, waiting for transfers between devices, shards(): lax.psum_scatter(placed_out, 'expert', scatter_dimension=1, tiled=True)  32.5 us
    dynamic_slice x1, local copies, waits for them, and re-layouts, shards(): mine_in = lax.dynamic_index_in_dim(in_split, half_index, 2, keepdims=False)  27.5 us
    all_to_all x1, starting transfers between devices, shards(): lax.all_to_all(send_rows, ('dp', 'tensor'), split_axis=0, concat_axis=0,...  15.4 us
  transfers between devices with their start and end apart: 9, of which 7 were waited for; matrix products, arithmetic and copies ran while one was open for 16% of the time, Pallas kernels for 0%

profile of v1, /device:TPU:1, one launch (start us, length us, event | category | flops | bytes accessed | tf_op | source)
XLA Modules:
  0.0 601.5 jit_solution(16592551732129783403)
XLA Ops:
  7.2 1.9 stack.2
  9.1 6.4 %all-to-all-start.2 = ((bf16[4,128,512]{2,1,0:T(8,128)(2,1)}), bf16[4,128,512]{2,1,0:T(8,128)(2,1)S(1)}, u32[]{:S(2)}, u32[]{:S(2)}) async-start(bf16[4,128,512]{2,1,0:T(8,128)(2,1)} %stack.2), calls=%async_computation.3 | async-start | bytes 1048576 | tf_op jit(solution)/shard_map/all_to_all | solution.py:80
  17.7 4.3 scatter_custom_fusion
  22.2 15.3 %all_gather.3 = bf16[128,2048]{1,0:T(8,128)(2,1)S(1)} all-gather(bf16[128,512]{1,0:T(8,128)(2,1)S(1)} %copy-done.8), channel_id=1, replica_groups=mesh['dp'=8,'tensor'=8,'expert'=4] {'expert'}, dimensions={1}, use_global_device_ids=true | all-gather | bytes 655360 | tf_op jit(solution)/shard_map/all_gather | solution.py:78
  37.8 4.2 gather_fusion
  42.1 6.1 %reshape.320 = bf16[64,12,2048]{2,1,0:T(8,128)(2,1)} reshape(bf16[768,2048]{1,0:T(8,128)(2,1)} %gather_fusion) | data formatting | bytes 6291456 | tf_op jit(solution)/shard_map/gather | solution.py:43
  48.2 4.5 broadcast_select_fusion
  52.7 15.4 %all-to-all-start = ((bf16[64,12,2048]{2,1,0:T(8,128)(2,1)}), bf16[64,12,2048]{2,1,0:T(8,128)(2,1)}, u32[]{:S(2)}, u32[]{:S(2)}) async-start(bf16[64,12,2048]{2,1,0:T(8,128)(2,1)} %broadcast_select_fusion), calls=%async_computation | async-start | bytes 8388608 | tf_op jit(solution)/shard_map/all_to_all | solution.py:92
  68.4 4.3 scatter_custom_fusion.1
  72.9 4.3 gather_fusion.2
  77.3 6.4 %reshape.371 = f32[64,12,2048]{2,1,0:T(8,128)} reshape(bf16[768,2048]{1,0:T(8,128)(2,1)} %gather_fusion.2) | data formatting | bytes 9437184 | tf_op jit(solution)/shard_map/convert_element_type | solution.py:45
  83.7 5.2 select_convert_fusion
  88.9 74.5 %all-to-all-done = bf16[64,12,2048]{2,1,0:T(8,128)(2,1)} async-done(((bf16[64,12,2048]{2,1,0:T(8,128)(2,1)}), bf16[64,12,2048]{2,1,0:T(8,128)(2,1)}, u32[]{:S(2)}, u32[]{:S(2)}) %all-to-all-start) | async-done | bytes 3145760 | tf_op jit(solution)/shard_map/all_to_all | solution.py:92
  163.4 8.2 %all-to-all-start.3 = ((bf16[64,12,2048]{2,1,0:T(8,128)(2,1)}), bf16[64,12,2048]{2,1,0:T(8,128)(2,1)}, u32[]{:S(2)}, u32[]{:S(2)}) async-start(bf16[64,12,2048]{2,1,0:T(8,128)(2,1)} %select_convert_fusion), calls=%async_computation.4 | async-start | bytes 8388608 | tf_op jit(solution)/shard_map/all_to_all | solution.py:93
  171.6 5.8 fusion.13
  177.5 5.2 fusion.17
  182.7 43.9 %all-to-all-done.3 = bf16[64,12,2048]{2,1,0:T(8,128)(2,1)} async-done(((bf16[64,12,2048]{2,1,0:T(8,128)(2,1)}), bf16[64,12,2048]{2,1,0:T(8,128)(2,1)}, u32[]{:S(2)}, u32[]{:S(2)}) %all-to-all-start.3) | async-done | bytes 3145760 | tf_op jit(solution)/shard_map/all_to_all | solution.py:93
  226.6 5.4 multiply_convert_fusion
  232.8 3.5 convolution_convert_fusion
  236.3 6.3 %reshape.307 = bf16[64,12,2,1024]{3,2,0,1:T(2,128)(2,1)} reshape(bf16[64,12,2048]{2,0,1:T(8,128)(2,1)} %convolution_convert_fusion) | data formatting | bytes 6291456 | tf_op jit(solution)/shard_map/reshape | solution.py:98
  242.6 1.8 fusion.15
  244.5 3.5 add_convert_fusion
  248.0 6.1 %reshape.313 = bf16[64,12,2,1024]{3,2,0,1:T(2,128)(2,1)} reshape(bf16[64,12,2048]{2,0,1:T(8,128)(2,1)} %add_convert_fusion) | data formatting | bytes 6291456 | tf_op jit(solution)/shard_map/reshape | solution.py:99
  254.1 27.5 %constant_dynamic-slice_fusion.1 = (bf16[64,12,1,1024]{3,2,0,1:T(2,128)(2,1)}, bf16[64,12,1,1024]{3,2,0,1:T(2,128)(2,1)}, bf16[64,12,1,1024]{3,2,0,1:T(2,128)(2,1)S(1)}, bf16[64,12,1,1024]{3,2,0,1:T(2,128)(2,1)S(1)}) fusion(bf16[64,12,2,1024]{3,2,0,1:T(2,128)(2,1)} %reshape.313, s32[]{:T(128)S(6)} %select_n.147, s32[]{:T(128)S(6)} %select_n.148, ...), kind=kLoop, calls=%fused_computation.96 | loop fusion | bytes 12582920 | tf_op jit(solution)/shard_map/jit(dynamic_index_in_dim)/dynamic_slice | solution.py:101
  282.2 37.1 %collective-permute-start = (bf16[64,12,1024]{2,0,1:T(8,128)(2,1)S(1)}, bf16[64,12,1024]{2,0,1:T(8,128)(2,1)S(1)}, u32[]{:S(2)}, u32[]{:S(2)}) collective-permute-start(bf16[64,12,1024]{2,0,1:T(8,128)(2,1)S(1)} %bitcast.104), channel_id=1, source_target_pairs={{0,1},{1,0},{2,3},{3,2},{4,5},{5,4},{6,7},{7,6},{8,9},{9,8},{10,11... | collective-permute-start | bytes 4718600 | tf_op jit(solution)/shard_map/ppermute | solution.py:8
  319.3 31.5 %collective-permute-done = bf16[64,12,1024]{2,0,1:T(8,128)(2,1)S(1)} collective-permute-done((bf16[64,12,1024]{2,0,1:T(8,128)(2,1)S(1)}, bf16[64,12,1024]{2,0,1:T(8,128)(2,1)S(1)}, u32[]{:S(2)}, u32[]{:S(2)}) %collective-permute-start) | collective-permute-done | bytes 1572896 | tf_op jit(solution)/shard_map/ppermute | solution.py:8
  351.9 2.2 copy.71
  354.1 13.4 %all-to-all-start.1 = ((bf16[64,12,1024]{2,1,0:T(8,128)(2,1)}), bf16[64,12,1024]{2,1,0:T(8,128)(2,1)}, u32[]{:S(2)}, u32[]{:S(2)}) async-start(bf16[64,12,1024]{2,1,0:T(8,128)(2,1)} %copy.71), calls=%async_computation.1 | async-start | bytes 4194304 | tf_op jit(solution)/shard_map/all_to_all | solution.py:108
  367.5 2.6 copy.137
  370.1 1.5 collective-permute-start.1
  371.7 76.4 %collective-permute-done.1 = bf16[64,12,1024]{2,0,1:T(8,128)(2,1)S(1)} collective-permute-done((bf16[64,12,1024]{2,0,1:T(8,128)(2,1)S(1)}, bf16[64,12,1024]{2,0,1:T(8,128)(2,1)S(1)}, u32[]{:S(2)}, u32[]{:S(2)}) %collective-permute-start.1) | collective-permute-done | bytes 1572896 | tf_op jit(solution)/shard_map/ppermute | solution.py:8
  449.1 2.2 copy.85
  451.3 13.4 %all-to-all-start.4 = ((bf16[64,12,1024]{2,1,0:T(8,128)(2,1)}), bf16[64,12,1024]{2,1,0:T(8,128)(2,1)}, u32[]{:S(2)}, u32[]{:S(2)}) async-start(bf16[64,12,1024]{2,1,0:T(8,128)(2,1)} %copy.85), calls=%async_computation.5 | async-start | bytes 4194304 | tf_op jit(solution)/shard_map/all_to_all | solution.py:109
  465.3 2.5 reshape.308
  467.8 5.4 gather_fusion.1
  473.2 2.9 fusion.1
  476.8 37.6 %all-to-all-done.4 = bf16[64,12,1024]{2,1,0:T(8,128)(2,1)} async-done(((bf16[64,12,1024]{2,1,0:T(8,128)(2,1)}), bf16[64,12,1024]{2,1,0:T(8,128)(2,1)}, u32[]{:S(2)}, u32[]{:S(2)}) %all-to-all-start.4) | async-done | bytes 1572896 | tf_op jit(solution)/shard_map/all_to_all | solution.py:109
  514.4 2.5 reshape.314
  516.9 5.4 gather_fusion.3
  522.3 2.9 fusion
  526.0 1.5 broadcast_select_fusion.1
  528.3 7.5 %fusion.6 = bf16[1,384,2048]{2,1,0:T(8,128)(2,1)} fusion(bf16[64,12,384]{2,0,1:T(8,128)(2,1)S(1)} %copy-done.13, bf16[64,12,2048]{2,1,0:T(8,128)(2,1)} %all-to-all-done.3), kind=kOutput, calls=%fused_computation.23 | convolution fusion | flops 1208745984 | bytes 5308416 | tf_op jit(solution)/shard_map/smh,smd->hd/dot_general | solution.py:34
  535.8 7.4 %fusion.5 = bf16[1,384,2048]{2,1,0:T(8,128)(2,1)} fusion(bf16[64,12,384]{2,0,1:T(8,128)(2,1)S(1)} %copy-done.7, bf16[64,12,2048]{2,1,0:T(8,128)(2,1)} %all-to-all-done), kind=kOutput, calls=%fused_computation.22 | convolution fusion | flops 1208745984 | bytes 5308416 | tf_op jit(solution)/shard_map/smh,smd->hd/dot_general | solution.py:31
  543.2 7.5 %fusion.4 = bf16[1,384,2048]{2,1,0:T(8,128)(2,1)} fusion(bf16[64,12,384]{2,0,1:T(8,128)(2,1)S(1)} %get-tuple-element.14, bf16[64,12,2048]{2,1,0:T(8,128)(2,1)} %all-to-all-done), kind=kOutput, calls=%fused_computation.21 | convolution fusion | flops 1208745984 | bytes 5308416 | tf_op jit(solution)/shard_map/smh,smd->hd/dot_general | solution.py:28
  550.7 7.9 %reduce-scatter.5.cloned.1.call-done = f32[128,512]{1,0:T(8,128)} async-done(((f32[128,2048]{1,0:T(8,128)}), f32[128,512]{1,0:T(8,128)}) %reduce-scatter.5.cloned.1.call-update) | async-done | bytes 262160 | tf_op jit(solution)/shard_map/reduce_scatter | solution.py:134
  558.6 1.6 convert_element_type.103
  560.2 32.5 %reduce-scatter.3.cloned.1.call-done = f32[128,512]{1,0:T(8,128)} async-done(((f32[128,2048]{1,0:T(8,128)}), f32[128,512]{1,0:T(8,128)}) %reduce-scatter.3.cloned.1.call-update) | async-done | bytes 262160 | tf_op jit(solution)/shard_map/reduce_scatter | solution.py:133
  592.7 1.6 convert_element_type.91
  (76 shorter events, 9.2 us)
Async XLA Ops:
  7.2 219.4 %copy-start = (bf16[1,384,2048]{2,1,0:T(8,128)(2,1)S(1)}, bf16[1,384,2048]{2,1,0:T(8,128)(2,1)}, u32[]{:S(2)}) copy-start(bf16[1,384,2048]{2,1,0:T(8,128)(2,1)} %param.15) | copy-start | bytes 4718596
  7.2 9.9 %copy-start.11 = (s32[128]{0:T(128)S(1)}, s32[128]{0:T(128)}, u32[]{:S(2)}) copy-start(s32[128]{0:T(128)} %param.12) | copy-start | bytes 1540
  7.2 15.0 %copy-start.8 = (bf16[128,512]{1,0:T(8,128)(2,1)S(1)}, bf16[128,512]{1,0:T(8,128)(2,1)}, u32[]{:S(2)}) copy-start(bf16[128,512]{1,0:T(8,128)(2,1)} %param.8) | copy-start | bytes 393220
  9.1 43.7 %all-to-all-start.2 = ((bf16[4,128,512]{2,1,0:T(8,128)(2,1)}), bf16[4,128,512]{2,1,0:T(8,128)(2,1)S(1)}, u32[]{:S(2)}, u32[]{:S(2)}) async-start(bf16[4,128,512]{2,1,0:T(8,128)(2,1)} %stack.2), calls=%async_computation.3 | async-start | bytes 1048576 | tf_op jit(solution)/shard_map/all_to_all | solution.py:80
  52.7 15.4 %copy-start.10 = (f32[128,8]{0,1:T(8,128)S(1)}, f32[128,8]{0,1:T(8,128)}, u32[]{:S(2)}) copy-start(f32[128,8]{0,1:T(8,128)} %param.11) | copy-start | bytes 12292
  52.7 110.6 %all-to-all-start = ((bf16[64,12,2048]{2,1,0:T(8,128)(2,1)}), bf16[64,12,2048]{2,1,0:T(8,128)(2,1)}, u32[]{:S(2)}, u32[]{:S(2)}) async-start(bf16[64,12,2048]{2,1,0:T(8,128)(2,1)} %broadcast_select_fusion), calls=%async_computation | async-start | bytes 8388608 | tf_op jit(solution)/shard_map/all_to_all | solution.py:92
  163.4 63.2 %all-to-all-start.3 = ((bf16[64,12,2048]{2,1,0:T(8,128)(2,1)}), bf16[64,12,2048]{2,1,0:T(8,128)(2,1)}, u32[]{:S(2)}, u32[]{:S(2)}) async-start(bf16[64,12,2048]{2,1,0:T(8,128)(2,1)} %select_convert_fusion), calls=%async_computation.4 | async-start | bytes 8388608 | tf_op jit(solution)/shard_map/all_to_all | solution.py:93
  171.6 5.9 copy-start.3
  232.0 0.8 copy-start.12
  232.0 12.4 %copy-start.6 = (bf16[64,12,384]{2,0,1:T(8,128)(2,1)}, bf16[64,12,384]{2,0,1:T(8,128)(2,1)S(1)}, u32[]{:S(2)}) copy-start(bf16[64,12,384]{2,0,1:T(8,128)(2,1)S(1)} %get-tuple-element.13) | copy-start | bytes 1769476
  236.3 6.3 %copy-start.4 = (bf16[1,384,2048]{2,1,0:T(8,128)(2,1)S(1)}, bf16[1,384,2048]{2,1,0:T(8,128)(2,1)}, u32[]{:S(2)}) copy-start(bf16[1,384,2048]{2,1,0:T(8,128)(2,1)} %param.13) | copy-start | bytes 4718596
  242.6 1.8 copy-start.5
  282.2 68.5 %collective-permute-start = (bf16[64,12,1024]{2,0,1:T(8,128)(2,1)S(1)}, bf16[64,12,1024]{2,0,1:T(8,128)(2,1)S(1)}, u32[]{:S(2)}, u32[]{:S(2)}) collective-permute-start(bf16[64,12,1024]{2,0,1:T(8,128)(2,1)S(1)} %bitcast.104), channel_id=1, source_target_pairs={{0,1},{1,0},{2,3},{3,2},{4,5},{5,4},{6,7},{7,6},{8,9},{9,8},{10,11... | collective-permute-start | bytes 4718600 | tf_op jit(solution)/shard_map/ppermute | solution.py:8
  354.1 97.3 %all-to-all-start.1 = ((bf16[64,12,1024]{2,1,0:T(8,128)(2,1)}), bf16[64,12,1024]{2,1,0:T(8,128)(2,1)}, u32[]{:S(2)}, u32[]{:S(2)}) async-start(bf16[64,12,1024]{2,1,0:T(8,128)(2,1)} %copy.71), calls=%async_computation.1 | async-start | bytes 4194304 | tf_op jit(solution)/shard_map/all_to_all | solution.py:108
  367.5 80.6 %copy-start.2 = (bf16[64,12,1,1024]{3,2,0,1:T(2,128)(2,1)S(1)}, bf16[64,12,1,1024]{3,2,0,1:T(2,128)(2,1)}, u32[]{:S(2)}) copy-start(bf16[64,12,1,1024]{3,2,0,1:T(2,128)(2,1)} %get-tuple-element.9) | copy-start | bytes 4718596
  370.1 77.9 %collective-permute-start.1 = (bf16[64,12,1024]{2,0,1:T(8,128)(2,1)S(1)}, bf16[64,12,1024]{2,0,1:T(8,128)(2,1)S(1)}, u32[]{:S(2)}, u32[]{:S(2)}) collective-permute-start(bf16[64,12,1024]{2,0,1:T(8,128)(2,1)S(1)} %bitcast.105), channel_id=1, source_target_pairs={{0,1},{1,0},{2,3},{3,2},{4,5},{5,4},{6,7},{7,6},{8,9},{9,8},{10,11... | collective-permute-start | bytes 4718600 | tf_op jit(solution)/shard_map/ppermute | solution.py:8
  449.1 15.8 %copy-start.9 = (s32[128,8]{0,1:T(8,128)S(1)}, s32[128,8]{0,1:T(8,128)}, u32[]{:S(2)}) copy-start(s32[128,8]{0,1:T(8,128)} %param.10) | copy-start | bytes 12292
  451.3 63.1 %all-to-all-start.4 = ((bf16[64,12,1024]{2,1,0:T(8,128)(2,1)}), bf16[64,12,1024]{2,1,0:T(8,128)(2,1)}, u32[]{:S(2)}, u32[]{:S(2)}) async-start(bf16[64,12,1024]{2,1,0:T(8,128)(2,1)} %copy.85), calls=%async_computation.5 | async-start | bytes 4194304 | tf_op jit(solution)/shard_map/all_to_all | solution.py:109
  464.8 93.8 %reduce-scatter.5.cloned.1.call-start = ((), (), s32[]{:S(2)}) async-start(), calls=%async_computation.8 | async-start | bytes 1310720 | tf_op jit(solution)/shard_map/reduce_scatter | solution.py:134
  525.9 2.3 copy-start.13
  527.5 65.2 %reduce-scatter.3.cloned.1.call-start = ((), (), s32[]{:S(2)}) async-start(), calls=%async_computation.7 | async-start | bytes 1310720 | tf_op jit(solution)/shard_map/reduce_scatter | solution.py:133
  528.3 7.5 %copy-start.7 = (bf16[64,12,384]{2,0,1:T(8,128)(2,1)S(1)}, bf16[64,12,384]{2,0,1:T(8,128)(2,1)}, u32[]{:S(2)}) copy-start(bf16[64,12,384]{2,0,1:T(8,128)(2,1)} %copy-done.6) | copy-start | bytes 1769476
  543.2 51.1 %copy-start.1 = (bf16[1,384,2048]{2,1,0:T(8,128)(2,1)S(1)}, bf16[1,384,2048]{2,1,0:T(8,128)(2,1)}, u32[]{:S(2)}) copy-start(bf16[1,384,2048]{2,1,0:T(8,128)(2,1)} %param.15) | copy-start | bytes 4718596
Sparse Core Ops, SparseCore 0:
  527.6 30.9 reduce-scatter.4
  561.3 31.3 reduce-scatter.2
